TPU v7x, 512 devices: a whole 4x4x16 slice. The times are simulated.
512 devices in a mesh: replica: 64 (over z, y_hi, core), shard: 8 (over x, y_lo).
Axes of the slice: x: 4, y: 4 (y_hi: 2, y_lo: 2; y = y_hi * 2 + y_lo), z: 16, core: 2. Of those that a mesh axis runs over, the one named last changes fastest.
Arguments:
- frames_in: bfloat16 [512, 512, 768], P(('replica', 'shard')), may hold values from -6 to 6
- lengths: int32 [512], P(('replica', 'shard')), may hold values from 128 to 512, as said below
- up_weight: bfloat16 [768, 1536], P('shard'), may hold values from -0.21875 to 0.21875
- norm_gain: bfloat16 [768], P('shard'), may hold values from 0.25 to 1.75
- conv_kernel: bfloat16 [32, 768], P(None, 'shard'), may hold values from -1 to 1
- down_weight: bfloat16 [768, 768], P(None, 'shard'), may hold values from -0.21875 to 0.21875
- cotangent: bfloat16 [512, 512, 768], P(('replica', 'shard')), may hold values from -24 to 24
Outputs:
- result: bfloat16 [512, 512, 768], P(('replica', 'shard'))
- grad_in: bfloat16 [512, 512, 768], P(('replica', 'shard'))
- up_grad: float32 [768, 1536], P('shard')
- gain_grad: float32 [768], P('shard')
- kernel_grad: float32 [32, 768], P(None, 'shard')
- down_grad: float32 [768, 768], P(None, 'shard')
Inputs may be any that keep to these rules, and one draw needn't show every extreme that they name: `lengths`: each length is a multiple of 128; utterance 0 has 512 frames.
All inputs are finite; a program needn't handle non-finite values.
Results may differ from a plain program's by a relative error of at most 0.017.
Values may be sent and summed in bfloat16 or wider, within the bound.
A program may use at most 64 MiB of HBM per device.

v0:
```python
import jax
import jax.numpy as jnp
from jax import lax
from jax.sharding import PartitionSpec as P

EPS = 1e-05


def normalize(inputs):
    average = jnp.mean(inputs, axis=1, keepdims=True)
    centred = inputs - average
    inv_std = lax.rsqrt(jnp.mean(centred * centred, axis=1, keepdims=True) + EPS)
    return (centred * inv_std, inv_std)


def depthwise(signal, taps_f, front, back):
    frames = signal.shape[1]
    padded = jnp.pad(signal, ((0, 0), (front, back), (0, 0)))
    total = jnp.zeros_like(signal)
    for offset in range(taps_f.shape[0]):
        total = total + taps_f[offset] * padded[:, offset : offset + frames]
    return total


def tap_grads(grad, signal, front, back):
    frames = signal.shape[1]
    padded = jnp.pad(signal, ((0, 0), (front, back), (0, 0)))
    return jnp.stack(
        [
            jnp.sum(grad * padded[:, offset : offset + frames], axis=(0, 1))
            for offset in range(front + back + 1)
        ]
    )


def body(frames_in, lengths, up_weight, norm_gain, conv_kernel, down_weight, cotangent):
    utts, frames, width = frames_in.shape
    chans = up_weight.shape[1] // 2
    count_taps = conv_kernel.shape[0]
    front = count_taps // 2
    back = count_taps - 1 - front
    row_count = utts * frames
    live = (jnp.arange(frames, dtype=jnp.int32)[None, :] < lengths[:, None]).astype(jnp.float32)
    live_col = live.reshape(row_count, 1)
    inputs = frames_in.reshape(row_count, width).astype(jnp.float32)
    normed, inv_std = normalize(inputs)
    up_full, gain_bf, taps_bf = (
        lax.all_gather(up_weight, "shard", axis=0, tiled=True),
        lax.all_gather(norm_gain, "shard", axis=0, tiled=True),
        lax.all_gather(conv_kernel, "shard", axis=1, tiled=True),
    )
    gain_f = gain_bf.astype(jnp.float32)
    scaled = (normed * gain_f).astype(jnp.bfloat16)
    projected = jnp.dot(scaled, up_full, preferred_element_type=jnp.float32)
    values_half = projected[:, :chans]
    gate_sig = jax.nn.sigmoid(projected[:, chans:])
    gated = (values_half * gate_sig * live_col).astype(jnp.bfloat16)
    taps_f = taps_bf.astype(jnp.float32)
    gated_f = gated.astype(jnp.float32).reshape(utts, frames, chans)
    filtered = depthwise(gated_f, taps_f, front, back).reshape(row_count, chans)
    activated = (jax.nn.silu(filtered) * live_col).astype(jnp.bfloat16)
    upstream = cotangent.reshape(row_count, width)
    down_full = lax.all_gather(down_weight, "shard", axis=1, tiled=True)
    mixed = jnp.dot(activated, down_full, preferred_element_type=jnp.float32)
    d_act = lax.dot_general(
        upstream, down_full, (((1,), (1,)), ((), ())), preferred_element_type=jnp.float32
    )
    result = (inputs + mixed).astype(jnp.bfloat16)
    down_part = lax.dot_general(
        activated, upstream, (((0,), (0,)), ((), ())), preferred_element_type=jnp.float32
    )
    factor = 1.0 / float(utts * lax.axis_size("replica") * lax.axis_size("shard") * frames) ** 0.5
    filt_sig = jax.nn.sigmoid(filtered)
    d_filt = d_act * live_col * filt_sig * (1.0 + filtered * (1.0 - filt_sig))
    d_filt3 = d_filt.reshape(utts, frames, chans)
    kernel_part = tap_grads(d_filt3, gated_f, front, back)
    d_gated = depthwise(d_filt3, taps_f[::-1], back, front).reshape(row_count, chans) * live_col
    d_proj = jnp.concatenate(
        [d_gated * gate_sig, d_gated * values_half * gate_sig * (1.0 - gate_sig)], axis=1
    ).astype(jnp.bfloat16)
    up_part = lax.dot_general(
        scaled, d_proj, (((0,), (0,)), ((), ())), preferred_element_type=jnp.float32
    )
    d_scaled = lax.dot_general(
        d_proj, up_full, (((1,), (1,)), ((), ())), preferred_element_type=jnp.float32
    )
    gain_part = jnp.sum(d_scaled * normed, axis=0)
    d_normed = d_scaled * gain_f
    d_inputs = inv_std * (
        d_normed
        - jnp.mean(d_normed, axis=1, keepdims=True)
        - normed * jnp.mean(d_normed * normed, axis=1, keepdims=True)
    )
    grad_in = (upstream.astype(jnp.float32) + d_inputs).astype(jnp.bfloat16)
    slices = (
        lax.psum_scatter(
            up_part.astype(jnp.bfloat16), "shard", scatter_dimension=0, tiled=True
        ).astype(jnp.float32),
        lax.psum_scatter(
            gain_part.astype(jnp.bfloat16), "shard", scatter_dimension=0, tiled=True
        ).astype(jnp.float32),
        lax.psum_scatter(
            kernel_part.astype(jnp.bfloat16), "shard", scatter_dimension=1, tiled=True
        ).astype(jnp.float32),
        lax.psum_scatter(
            down_part.astype(jnp.bfloat16), "shard", scatter_dimension=1, tiled=True
        ).astype(jnp.float32),
    )
    up_total, gain_total, kernel_total, down_total = lax.psum(
        (slices[0], slices[1], slices[2], slices[3]), "replica"
    )
    return (
        result.reshape(utts, frames, width),
        grad_in.reshape(utts, frames, width),
        up_total * factor,
        gain_total * factor,
        kernel_total * factor,
        down_total * factor,
    )


def solution(mesh):
    return jax.shard_map(
        body,
        mesh=mesh,
        in_specs=(
            P(("replica", "shard"), None, None),
            P(("replica", "shard")),
            P("shard", None),
            P("shard"),
            P(None, "shard"),
            P(None, "shard"),
            P(("replica", "shard"), None, None),
        ),
        out_specs=(
            P(("replica", "shard"), None, None),
            P(("replica", "shard"), None, None),
            P("shard", None),
            P("shard"),
            P(None, "shard"),
            P(None, "shard"),
        ),
        check_vma=False,
    )
```

profile of v0, /device:TPU:6, one launch (start us, length us, event | category | flops | bytes accessed | tf_op | source)
XLA Modules:
  0.0 580.0 jit_solution(7954746644922215602)
XLA Ops:
  7.2 0.7 all-gather.4.cloned.1.call-update
  8.0 0.7 all-gather.6.cloned.1.call-update
  8.7 34.6 %all-gather = bf16[8,96,32]{1,2,0:T(8,128)(2,1)S(1)} all-gather(bf16[1,96,32]{1,2,0:T(8,128)(2,1)} %bitcast.209), channel_id=1, replica_groups=mesh['replica'=64,'shard'=8] {'shard'}, dimensions={0}, use_global_device_ids=true | all-gather | bytes 55296 | tf_op jit(solution)/shard_map/all_gather | solution.py:50
  45.0 0.6 fusion.79
  46.5 14.7 %all-reduce.2 = bf16[768]{0:T(1024)(128)(2,1)S(1)} all-reduce(bf16[768]{0:T(1024)(128)(2,1)S(1)} %dynamic-update-slice), channel_id=1, replica_groups=mesh['replica'=64,'shard'=8] {'shard'}, use_global_device_ids=true, to_apply=%add.2 | all-reduce | flops 768 | bytes 3072
  61.2 18.4 %all-gather.4.cloned.1.call-done = bf16[768,1536]{1,0:T(8,128)(2,1)} async-done(((bf16[96,1536]{1,0:T(8,128)(2,1)}), bf16[768,1536]{1,0:T(8,128)(2,1)}) %all-gather.4.cloned.1.call-update) | async-done | bytes 2359312 | tf_op jit(solution)/shard_map/all_gather | solution.py:48
  79.6 3.1 fusion.77
  83.2 1.2 copy-done
  84.4 0.9 copy-done.4
  85.3 7.4 %fusion.33 = f32[1,512,768]{2,1,0:T(8,128)} fusion(bf16[512,768]{1,0:T(8,128)(2,1)S(1)} %get-tuple-element.79, f32[768]{0:T(1024)S(1)} %get-tuple-element.41, f32[768]{0:T(1024)S(1)} %get-tuple-element.42, f32[768]{0:T(1024)S(1)} %get-tuple-element.43, f32[768]{0:T(1024)S(1)} %get-tuple-element.44, f32[768]{0:T(1024)S(1)} %get-tuple-element.45, ...), kind=kLoop, calls=%fused_computation.39 | loop fusion | flops 25165824 | bytes 4030464 | tf_op jit(solution)/shard_map/add | solution.py:21
  92.7 34.8 %all-gather.6.cloned.1.call-done = bf16[768,768]{0,1:T(8,128)(2,1)} async-done(((bf16[768,96]{0,1:T(8,128)(2,1)}), bf16[768,768]{0,1:T(8,128)(2,1)}) %all-gather.6.cloned.1.call-update) | async-done | bytes 1179664 | tf_op jit(solution)/shard_map/all_gather | solution.py:63
  127.5 5.7 multiply_reduce_fusion.1
  133.2 4.1 multiply_reduce_fusion
  138.2 0.8 copy.15
  139.1 3.2 convolution_convert_fusion.1
  142.6 9.2 %multiply_convert_fusion.2 = (bf16[512,768]{1,0:T(8,128)(2,1)S(1)}, f32[512,768]{1,0:T(8,128)S(1)}) fusion(f32[512,1536]{1,0:T(8,128)} %copy-done, f32[512]{0:T(512)S(1)} %fusion.71, f32[768]{0:T(1024)S(1)} %get-tuple-element.40, f32[768]{0:T(1024)S(1)} %get-tuple-element.59, f32[768]{0:T(1024)S(1)} %get-tuple-element.71, f32[768]{0:T(1024)S(1)} %get-tuple-element.70, ...), kind=kLoop, calls=%fused_computation.107 | loop fusion | flops 27131904 | bytes 7178240 | tf_op jit(solution)/shard_map/convert.64
  152.7 0.5 copy-done.10
  153.3 3.0 convolution_convert_fusion
  157.0 3.9 fusion.14
  160.8 16.3 %all-reduce.3 = bf16[768]{0:T(1024)(128)(2,1)S(1)} all-reduce(bf16[768]{0:T(1024)(128)(2,1)S(1)} %get-tuple-element.37), channel_id=3, replica_groups=mesh['replica'=64,'shard'=8] {'shard'}, use_global_device_ids=true, to_apply=%region_7.8.clone | all-reduce | flops 768 | bytes 3072
  177.2 1.5 fusion.64
  178.7 0.5 copy-done.12
  179.2 1.9 fusion.62
  181.2 1.5 reduce-scatter.10.cloned.1.call-done
  182.7 0.8 copy.16
  183.5 49.3 %reduce-scatter.8.cloned.1.call-done = bf16[768,96]{0,1:T(8,128)(2,1)} async-done(((bf16[768,768]{0,1:T(8,128)(2,1)}), bf16[768,96]{0,1:T(8,128)(2,1)}) %reduce-scatter.8.cloned.1.call-update) | async-done | bytes 147472 | tf_op jit(solution)/shard_map/reduce_scatter | solution.py:105
  232.8 68.0 %reduce-scatter.6.cloned.1.call-done = bf16[96,1536]{1,0:T(8,128)(2,1)} async-done(((bf16[768,1536]{1,0:T(8,128)(2,1)}), bf16[96,1536]{1,0:T(8,128)(2,1)}) %reduce-scatter.6.cloned.1.call-update) | async-done | bytes 294928 | tf_op jit(solution)/shard_map/reduce_scatter | solution.py:96
  300.8 269.9 %all-reduce.6 = (f32[96,1536]{1,0:T(8,128)S(1)}, f32[96]{0:T(128)S(1)}, f32[32,96]{1,0:T(8,128)S(1)}, f32[768,96]{0,1:T(8,128)S(1)}) all-reduce(bf16[96,1536]{1,0:T(8,128)(2,1)} %reduce-scatter.6.cloned.1.call-done, f32[96]{0:T(128)S(1)} %dynamic-slice_convert_fusion, ...), channel_id=1, replica_groups=mesh['replica'=64,'shard'=8] {'replica'}, use_global_device_ids=true, to_apply=%region_5.6 | all-reduce | flops 224352 | bytes 1346304 | tf_op jit(solution)/shard_map/psum | solution.py:109
  570.7 0.9 broadcast_multiply_fusion
  571.6 0.7 broadcast_multiply_fusion.1
  572.3 0.6 broadcast_multiply_fusion.2
  573.0 0.5 broadcast_multiply_fusion.6
  (82 shorter events, 3.7 us)
Async XLA Ops:
  7.2 37.9 %copy-start.11 = (u32[512]{0:T(512)S(1)}, u32[512]{0:T(512)}, u32[]{:S(2)}) copy-start(u32[512]{0:T(512)} %constant.30) | copy-start | bytes 6148
  7.2 36.6 %copy-start.2 = (bf16[1,512,768]{2,1,0:T(8,128)(2,1)S(1)}, bf16[1,512,768]{2,1,0:T(8,128)(2,1)}, u32[]{:S(2)}) copy-start(bf16[1,512,768]{2,1,0:T(8,128)(2,1)} %param.7) | copy-start | bytes 2359300
  7.2 39.1 %copy-start.13 = (bf16[96]{0:T(256)(128)(2,1)S(1)}, bf16[96]{0:T(256)(128)(2,1)}, u32[]{:S(2)}) copy-start(bf16[96]{0:T(256)(128)(2,1)} %param.10) | copy-start | bytes 580
  7.2 72.4 %all-gather.4.cloned.1.call-start = ((), (), s32[]{:S(2)}) async-start(), calls=%async_computation.3 | async-start | bytes 2654208 | tf_op jit(solution)/shard_map/all_gather | solution.py:48
  7.9 119.6 %all-gather.6.cloned.1.call-start = ((), (), s32[]{:S(2)}) async-start(), calls=%async_computation.4 | async-start | bytes 1327104 | tf_op jit(solution)/shard_map/all_gather | solution.py:63
  8.7 174.0 %reduce-scatter.10.cloned.1.call-start = ((), (), s32[]{:S(2)}) async-start(), calls=%async_computation.7 | async-start | bytes 221184
  82.8 1.7 copy-start
  84.4 0.9 copy-start.4
  133.2 4.1 copy-start.5
  137.3 1.8 copy-start.6
  139.0 93.7 %reduce-scatter.8.cloned.1.call-start = ((), (), s32[]{:S(2)}) async-start(), calls=%async_computation.6 | async-start | bytes 1327104 | tf_op jit(solution)/shard_map/reduce_scatter | solution.py:105
  142.3 158.5 %reduce-scatter.6.cloned.1.call-start = ((), (), s32[]{:S(2)}) async-start(), calls=%async_computation.5 | async-start | bytes 2654208 | tf_op jit(solution)/shard_map/reduce_scatter | solution.py:96
  142.6 9.2 %copy-start.1 = (f32[512,1536]{1,0:T(8,128)S(1)}, f32[512,1536]{1,0:T(8,128)}, u32[]{:S(2)}) copy-start(f32[512,1536]{1,0:T(8,128)} %copy-done) | copy-start | bytes 9437188
  151.8 0.9 copy-start.9
  151.8 1.4 copy-start.3
  152.3 0.9 copy-start.10
  156.9 20.3 %copy-start.8 = (bf16[1,512,768]{2,1,0:T(8,128)(2,1)S(1)}, bf16[1,512,768]{2,1,0:T(8,128)(2,1)}, u32[]{:S(2)}) copy-start(bf16[1,512,768]{2,1,0:T(8,128)(2,1)} %param.13) | copy-start | bytes 2359300
  177.2 1.5 copy-start.7
  177.2 2.0 copy-start.12
Sparse Core Ops, SparseCore 0:
  10.1 69.4 all-gather.3
  81.7 45.7 all-gather.5
  139.2 43.4 reduce-scatter.9
  185.6 47.1 reduce-scatter.7
  235.7 65.0 reduce-scatter.5
where the time goes:
time: 580 us
  blocking collectives  336 us (58%)
  waiting for transfers between devices  173 us (30%)
  other arithmetic  26.7 us (5%)
  matrix products  20.9 us (4%)
  between operations  16.2 us (3%)
  local copies, waits for them, and re-layouts  6.83 us (1%)
    psum x1, blocking collectives, body(): lax.psum((slices[0], slices[1], slices[2], slices[3]), 'replica')  270 us
    reduce_scatter x1, waiting for transfers between devices, body(): lax.psum_scatter(up_part.astype(jnp.bfloat16), 'shard', scatter_dimension...  68 us
    reduce_scatter x1, waiting for transfers between devices, body(): lax.psum_scatter(down_part.astype(jnp.bfloat16), 'shard', scatter_dimensi...  49.3 us
    all_gather x1, waiting for transfers between devices, body(): down_full = lax.all_gather(down_weight, 'shard', axis=1, tiled=True)  34.8 us
    all_gather x1, blocking collectives, body(): lax.all_gather(conv_kernel, 'shard', axis=1, tiled=True)  34.6 us
    unnamed x2, blocking collectives  31 us
    all_gather x1, waiting for transfers between devices, body(): lax.all_gather(up_weight, 'shard', axis=0, tiled=True)  18.4 us
  transfers between devices with their start and end apart: 5, of which 5 were waited for; matrix products, arithmetic and copies ran while one was open for 6% of the time, Pallas kernels for 0%

commit v1 on v0

--- a/solution.py
+++ b/solution.py
@@ -45,7 +45,9 @@
     inputs = frames_in.reshape(row_count, width).astype(jnp.float32)
     normed, inv_std = normalize(inputs)
     up_full, gain_bf, taps_bf = (
-        lax.all_gather(up_weight, "shard", axis=0, tiled=True),
+        jnp.concatenate(
+            lax.all_to_all(jnp.stack([up_weight] * lax.axis_size("shard")), "shard", 0, 0), axis=0
+        ),
         lax.all_gather(norm_gain, "shard", axis=0, tiled=True),
         lax.all_gather(conv_kernel, "shard", axis=1, tiled=True),
     )

time: 580 us -> 560 us (0.966)
  waiting for transfers between devices: 173 us -> 124 us
  blocking collectives: 336 us -> 350 us
  starting transfers between devices: 0.38 us -> 9.87 us
    all_gather x1, waiting for transfers between devices: 34.8 us -> 0.01 us  [body(): down_full = lax.all_gather(down_weight, 'shard', axis=1, tiled=True)]
    all_gather x1 -> x0, waiting for transfers between devices: 18.4 us -> none  [body(): lax.all_gather(up_weight, 'shard', axis=0, tiled=True)]
    all_gather x1, blocking collectives: 34.6 us -> 47.3 us  [body(): lax.all_gather(conv_kernel, 'shard', axis=1, tiled=True)]
    all_to_all x0 -> x1, starting transfers between devices: none -> 9.53 us  [body(): lax.all_to_all(jnp.stack([up_weight] * lax.axis_size('shard')), 'shard',...]
  transfers between devices with their start and end apart: 5 -> 5, of which waited for: 5 -> 3; matrix products, arithmetic and copies ran while one was open for 6% -> 7% of each run, Pallas kernels for 0% -> 0%
where the time goes in v1:
time: 560 us; the launch traced here: 559 us
  blocking collectives  350 us (62%)
  waiting for transfers between devices  124 us (22%)
  other arithmetic  28.5 us (5%)
  matrix products  19.5 us (3%)
  between operations  16.3 us (3%)
  local copies, waits for them, and re-layouts  11.2 us (2%)
  starting transfers between devices  9.87 us (2%)
    psum x1, blocking collectives, body(): lax.psum((slices[0], slices[1], slices[2], slices[3]), 'replica')  270 us
    reduce_scatter x1, waiting for transfers between devices, body(): lax.psum_scatter(up_part.astype(jnp.bfloat16), 'shard', scatter_dimension...  67.9 us
    reduce_scatter x1, waiting for transfers between devices, body(): lax.psum_scatter(down_part.astype(jnp.bfloat16), 'shard', scatter_dimensi...  49.4 us
    all_gather x1, blocking collectives, body(): lax.all_gather(conv_kernel, 'shard', axis=1, tiled=True)  47.3 us
    unnamed x2, blocking collectives  32.8 us
  transfers between devices with their start and end apart: 5, of which 3 were waited for; matrix products, arithmetic and copies ran while one was open for 7% of the time, Pallas kernels for 0%

profile of v1, /device:TPU:6, one launch (start us, length us, event | category | flops | bytes accessed | tf_op | source)
XLA Modules:
  0.0 559.1 jit_solution(2266948848682012421)
XLA Ops:
  7.2 2.6 stack.143
  9.7 9.5 %all-to-all-start = ((bf16[8,96,1536]{2,1,0:T(8,128)(2,1)}), bf16[8,96,1536]{2,1,0:T(8,128)(2,1)S(1)}, u32[]{:S(2)}, u32[]{:S(2)}) async-start(bf16[8,96,1536]{2,1,0:T(8,128)(2,1)} %stack.143), calls=%async_computation | async-start | bytes 4718592 | tf_op jit(solution)/shard_map/all_to_all | solution.py:49
  19.3 0.7 all-gather.3.cloned.1.call-update
  20.7 47.3 %all-gather = bf16[8,96,32]{1,2,0:T(8,128)(2,1)S(1)} all-gather(bf16[1,96,32]{1,2,0:T(8,128)(2,1)S(1)} %bitcast.214), channel_id=1, replica_groups=mesh['replica'=64,'shard'=8] {'shard'}, dimensions={0}, use_global_device_ids=true | all-gather | bytes 55296 | tf_op jit(solution)/shard_map/all_gather | solution.py:52
  69.0 0.6 fusion.89
  70.5 15.7 %all-reduce.2 = bf16[768]{0:T(1024)(128)(2,1)S(1)} all-reduce(bf16[768]{0:T(1024)(128)(2,1)S(1)} %dynamic-update-slice), channel_id=1, replica_groups=mesh['replica'=64,'shard'=8] {'shard'}, use_global_device_ids=true, to_apply=%add.2 | all-reduce | flops 768 | bytes 3072
  86.3 1.4 copy-done.6
  87.7 1.5 fusion.68
  89.7 1.2 copy-done
  90.9 0.9 copy-done.4
  91.8 7.4 %fusion.36 = f32[1,512,768]{2,1,0:T(8,128)} fusion(bf16[512,768]{1,0:T(8,128)(2,1)S(1)} %get-tuple-element.79, f32[768]{0:T(1024)S(1)} %get-tuple-element.41, f32[768]{0:T(1024)S(1)} %get-tuple-element.42, f32[768]{0:T(1024)S(1)} %get-tuple-element.43, f32[768]{0:T(1024)S(1)} %get-tuple-element.44, f32[768]{0:T(1024)S(1)} %get-tuple-element.45, ...), kind=kLoop, calls=%fused_computation.43 | loop fusion | flops 25165824 | bytes 4030464 | tf_op jit(solution)/shard_map/add | solution.py:21
  99.2 5.7 %multiply_reduce_fusion.1 = (bf16[768]{0:T(1024)(128)(2,1)S(1)}, bf16[768]{0:T(1024)(128)(2,1)S(1)}, bf16[768]{0:T(1024)(128)(2,1)S(1)}, bf16[768]{0:T(1024)(128...) fusion(f32[1,512,768]{2,1,0:T(8,128)S(1)} %get-tuple-element.78, ...), kind=kOutput, calls=%fused_computation.80 | convolution fusion | flops 617732352 | bytes 6706688 | tf_op jit(solution)/shard_map/dot_general | solution.py:67
  104.9 4.1 multiply_reduce_fusion
  109.9 0.8 copy.15
  110.8 3.2 convolution_convert_fusion.1
  114.3 9.2 %multiply_convert_fusion.2 = (bf16[512,768]{1,0:T(8,128)(2,1)S(1)}, f32[512,768]{1,0:T(8,128)S(1)}) fusion(f32[512,1536]{1,0:T(8,128)} %copy-done, f32[512]{0:T(512)S(1)} %fusion.84, f32[768]{0:T(1024)S(1)} %get-tuple-element.40, f32[768]{0:T(1024)S(1)} %get-tuple-element.59, f32[768]{0:T(1024)S(1)} %get-tuple-element.71, f32[768]{0:T(1024)S(1)} %get-tuple-element.70, ...), kind=kLoop, calls=%fused_computation.111 | loop fusion | flops 27131904 | bytes 7178240 | tf_op jit(solution)/shard_map/convert.64
  124.3 0.5 copy-done.11
  124.9 3.0 convolution_convert_fusion
  128.8 0.9 copy-done.7
  129.6 4.1 fusion.14
  133.7 17.1 %all-reduce.3 = bf16[768]{0:T(1024)(128)(2,1)S(1)} all-reduce(bf16[768]{0:T(1024)(128)(2,1)S(1)} %get-tuple-element.37), channel_id=3, replica_groups=mesh['replica'=64,'shard'=8] {'shard'}, use_global_device_ids=true, to_apply=%region_7.8.clone | all-reduce | flops 768 | bytes 3072
  150.9 3.3 fusion.71
  154.1 2.0 fusion.65
  156.1 6.1 %reduce-scatter.10.cloned.1.call-done = bf16[96,32]{1,0:T(8,128)(2,1)} async-done(((bf16[768,32]{1,0:T(8,128)(2,1)}), bf16[96,32]{1,0:T(8,128)(2,1)}) %reduce-scatter.10.cloned.1.call-update) | async-done | bytes 6160
  162.2 0.8 copy.16
  163.0 49.4 %reduce-scatter.8.cloned.1.call-done = bf16[768,96]{0,1:T(8,128)(2,1)} async-done(((bf16[768,768]{0,1:T(8,128)(2,1)}), bf16[768,96]{0,1:T(8,128)(2,1)}) %reduce-scatter.8.cloned.1.call-update) | async-done | bytes 147472 | tf_op jit(solution)/shard_map/reduce_scatter | solution.py:107
  212.4 67.9 %reduce-scatter.6.cloned.1.call-done = bf16[96,1536]{1,0:T(8,128)(2,1)} async-done(((bf16[768,1536]{1,0:T(8,128)(2,1)}), bf16[96,1536]{1,0:T(8,128)(2,1)}) %reduce-scatter.6.cloned.1.call-update) | async-done | bytes 294928 | tf_op jit(solution)/shard_map/reduce_scatter | solution.py:98
  280.3 269.5 %all-reduce.6 = (f32[96,1536]{1,0:T(8,128)S(1)}, f32[96]{0:T(128)S(1)}, f32[32,96]{1,0:T(8,128)S(1)}, f32[768,96]{0,1:T(8,128)S(1)}) all-reduce(bf16[96,1536]{1,0:T(8,128)(2,1)} %reduce-scatter.6.cloned.1.call-done, f32[96]{0:T(128)S(1)} %dynamic-slice_convert_fusion, ...), channel_id=1, replica_groups=mesh['replica'=64,'shard'=8] {'replica'}, use_global_device_ids=true, to_apply=%region_5.6 | all-reduce | flops 224352 | bytes 1346304 | tf_op jit(solution)/shard_map/psum | solution.py:111
  549.8 0.9 broadcast_multiply_fusion
  550.7 0.7 broadcast_multiply_fusion.1
  551.4 0.6 broadcast_multiply_fusion.2
  552.0 0.5 broadcast_multiply_fusion.6
  (86 shorter events, 3.7 us)
Async XLA Ops:
  9.7 11.0 %copy-start.12 = (bf16[32,96]{1,0:T(8,128)(2,1)S(1)}, bf16[32,96]{1,0:T(8,128)(2,1)}, u32[]{:S(2)}) copy-start(bf16[32,96]{1,0:T(8,128)(2,1)} %param.11) | copy-start | bytes 18436
  9.7 58.7 %copy-start.2 = (bf16[1,512,768]{2,1,0:T(8,128)(2,1)S(1)}, bf16[1,512,768]{2,1,0:T(8,128)(2,1)}, u32[]{:S(2)}) copy-start(bf16[1,512,768]{2,1,0:T(8,128)(2,1)} %param.7) | copy-start | bytes 2359300
  9.7 76.5 %all-to-all-start = ((bf16[8,96,1536]{2,1,0:T(8,128)(2,1)}), bf16[8,96,1536]{2,1,0:T(8,128)(2,1)S(1)}, u32[]{:S(2)}, u32[]{:S(2)}) async-start(bf16[8,96,1536]{2,1,0:T(8,128)(2,1)} %stack.143), calls=%async_computation | async-start | bytes 4718592 | tf_op jit(solution)/shard_map/all_to_all | solution.py:49
  19.3 49.7 %copy-start.13 = (u32[512]{0:T(512)S(1)}, u32[512]{0:T(512)}, u32[]{:S(2)}) copy-start(u32[512]{0:T(512)} %constant.30) | copy-start | bytes 6148
  19.3 51.0 %copy-start.15 = (bf16[96]{0:T(256)(128)(2,1)S(1)}, bf16[96]{0:T(256)(128)(2,1)}, u32[]{:S(2)}) copy-start(bf16[96]{0:T(256)(128)(2,1)} %param.10) | copy-start | bytes 580
  19.3 79.9 %all-gather.3.cloned.1.call-start = ((), (), s32[]{:S(2)}) async-start(), calls=%async_computation.4 | async-start | bytes 1327104 | tf_op jit(solution)/shard_map/all_gather | solution.py:65
  20.0 142.2 %reduce-scatter.10.cloned.1.call-start = ((), (), s32[]{:S(2)}) async-start(), calls=%async_computation.7 | async-start | bytes 221184
  86.3 1.4 copy-start.6
  89.2 1.7 copy-start
  90.9 0.9 copy-start.4
  104.9 4.1 copy-start.5
  109.0 1.8 copy-start.8
  110.7 101.7 %reduce-scatter.8.cloned.1.call-start = ((), (), s32[]{:S(2)}) async-start(), calls=%async_computation.6 | async-start | bytes 1327104 | tf_op jit(solution)/shard_map/reduce_scatter | solution.py:107
  114.0 166.3 %reduce-scatter.6.cloned.1.call-start = ((), (), s32[]{:S(2)}) async-start(), calls=%async_computation.5 | async-start | bytes 2654208 | tf_op jit(solution)/shard_map/reduce_scatter | solution.py:98
  114.2 9.2 %copy-start.1 = (f32[512,1536]{1,0:T(8,128)S(1)}, f32[512,1536]{1,0:T(8,128)}, u32[]{:S(2)}) copy-start(f32[512,1536]{1,0:T(8,128)} %copy-done) | copy-start | bytes 9437188
  123.5 0.9 copy-start.10
  123.5 1.4 copy-start.3
  124.0 0.9 copy-start.11
  127.9 1.7 copy-start.7
  150.9 3.3 copy-start.9
  150.9 3.3 copy-start.14
Sparse Core Ops, SparseCore 0:
  22.2 47.6 all-gather.2
  110.8 51.3 reduce-scatter.9
  165.3 47.0 reduce-scatter.7
  215.4 64.8 reduce-scatter.5
